TPU v7x, 32 devices: a whole 2x2x4 slice. The times are simulated.
32 devices in a mesh: groups: 2 (over x), ctx: 16 (over z, y, core).
Axes of the slice: x: 2, y: 2, z: 4, core: 2. Of those that a mesh axis runs over, the one named last changes fastest.
Arguments:
- queries: bfloat16 [4096, 8192], P(('groups', 'ctx')), parts along dimension 0, may hold values from -8 to 8
- new_keys: bfloat16 [4096, 1024], P(('groups', 'ctx')), parts along dimension 0, may hold values from -12 to 12
- new_values: bfloat16 [4096, 1024], P(('groups', 'ctx')), parts along dimension 0, may hold values from -6 to 6
- prefix_keys: bfloat16 [256, 1024], P(('groups', 'ctx')), parts along dimension 0, may hold values from -16 to 16
- prefix_values: bfloat16 [256, 1024], P(('groups', 'ctx')), parts along dimension 0, may hold values from -6 to 6
- pool_keys: bfloat16 [32, 2, 256, 1024], P(('groups', 'ctx')), parts along dimension 0, may hold values from -12 to 12
- pool_values: bfloat16 [32, 2, 256, 1024], P(('groups', 'ctx')), parts along dimension 0, may hold values from -6 to 6
- owners: int32 [4], P('groups'), parts along dimension 0, may hold values from 0 to 15
- lengths: int32 [32], P(('groups', 'ctx')), parts along dimension 0, may hold values from 1 to 128, as said below
Outputs:
- attended: bfloat16 [4096, 8192], P(('groups', 'ctx')), parts along dimension 0
There are 2 independent parts, one for each index of `groups`. A program takes and returns all parts, laid end to end along the dimension named above; each array names one. Nothing has to cross between parts.
Inputs may be any that keep to these rules, and one draw needn't show every extreme that they name: `lengths`: some device's prompt fills all 128 slots.
All inputs are finite; a program needn't handle non-finite values.
Results may differ from a plain program's by a relative error of at most 0.0035.
Values may be sent and summed in bfloat16 or wider, within the bound.
A program may use at most 128 MiB of HBM per device.

v0:
```python
import functools

import jax
import jax.numpy as jnp
from jax import lax
from jax.experimental import pallas as pl
from jax.experimental.pallas import tpu as pltpu
from jax.sharding import PartitionSpec as P

HD = 128
SIB_STEPS = 1
HOP_STEPS = 3
CUTS = 1
HEADS_AT_ONCE = 4
SUB = 2


def grid_of(ring):
    chips = ring // 2
    short = 1
    while (short * 2) ** 2 <= chips and chips % (short * 2) == 0:
        short *= 2
    return chips // short, short


def kernel(
    ring, heads, kv_heads,
    q_hbm, nk_ref, nv_ref, pk_ref, pv_ref, poolk_ref, poolv_ref, owners_ref, lengths_ref,
    out_hbm,
    x, sib_s, sib_r, in_up, in_dn, up_s, up_r, dn_s, dn_r, kvf, bias, q_ref, out_ref,
    send_sems, recv_sems, q_sem, out_sems,
):
    long, short = grid_of(ring)
    me = lax.axis_index("ctx")
    core = lax.rem(me, 2)
    chip = lax.div(me, 2)
    py = lax.rem(chip, short)
    pz = lax.div(chip, short)
    sibling = me + 1 - 2 * core
    pieces = poolk_ref.shape[1] * CUTS
    blk = poolk_ref.shape[2] // CUTS
    chunks = kv_heads * pieces
    own_rows = pk_ref.shape[0]
    pre = own_rows * ring // pieces
    rows = q_hbm.shape[0]
    group = heads // kv_heads

    q_copy = pltpu.make_async_copy(q_hbm, q_ref, q_sem)
    q_copy.start()
    barrier = pltpu.get_barrier_semaphore()

    def greet(target):
        pl.semaphore_signal(barrier, inc=1, device_id={"ctx": target})

    greet(sibling)
    for pos, size, step in ((py, short, 2), (pz, long, 2 * short)):
        @pl.when(pos > 0)
        def _():
            greet(me - step)

        @pl.when(pos < size - 1)
        def _():
            greet(me + step)

    peers = 1
    for pos, size in ((py, short), (pz, long)):
        peers = peers + jnp.where(pos > 0, 1, 0) + jnp.where(pos < size - 1, 1, 0)
    pl.semaphore_wait(barrier, peers)

    def remote(kind, i, src, dst, target):
        return pltpu.make_async_remote_copy(
            src_ref=src, dst_ref=dst, send_sem=send_sems.at[kind, i], recv_sem=recv_sems.at[kind, i],
            device_id={"ctx": target}, device_id_type=pl.DeviceIdType.MESH,
        )

    length = lengths_ref[0]
    tok = lax.broadcasted_iota(jnp.int32, (rows, rows), 0)
    key = lax.broadcasted_iota(jnp.int32, (rows, rows), 1)
    bias[...] = jnp.where((key <= tok) & (key < length), 0.0, -1e30)

    def cols(g):
        return pl.ds(pl.multiple_of(g * HD, HD), HD)

    def build(i):
        g, b = lax.div(i, pieces), lax.rem(i, pieces)
        page_of = lax.div(b, CUTS)
        start = pl.multiple_of(lax.rem(b, CUTS) * blk, blk)
        mine = jnp.where(owners_ref[page_of] == me, 1.0, 0.0).astype(jnp.float32)
        row = lax.broadcasted_iota(jnp.int32, (pre, HD), 0) + b * pre
        in_mine = (row >= me * own_rows) & (row < (me + 1) * own_rows)
        parts = []
        for pool, pre_ref in ((poolk_ref, pk_ref), (poolv_ref, pv_ref)):
            page = pool[0, page_of, pl.ds(start, blk), cols(g)]
            page = page * jnp.full(page.shape, mine, jnp.float32).astype(jnp.bfloat16)
            mine_pre = pre_ref[:, cols(g)].astype(jnp.float32)
            tiled = jnp.concatenate([mine_pre] * (pre // own_rows), axis=0)
            parts.append((page, jnp.where(in_mine, tiled, 0.0).astype(jnp.bfloat16)))
        is_k = core == 0

        @pl.when(is_k)
        def _():
            x[i, :blk], x[i, blk:] = parts[0]
            sib_s[i, :blk], sib_s[i, blk:] = parts[1]

        @pl.when(jnp.logical_not(is_k))
        def _():
            x[i, :blk], x[i, blk:] = parts[1]
            sib_s[i, :blk], sib_s[i, blk:] = parts[0]

    def valid(i):
        return (i >= 0) & (i < chunks)

    first_is_y = core == 0

    def pick(if_y, if_z):
        return jnp.where(first_is_y, if_y, if_z)

    p1, l1, s1 = pick(py, pz), pick(short, long), pick(2, 2 * short)
    p2, l2, s2 = pick(pz, py), pick(long, short), pick(2 * short, 2)
    depth = lax.div(l1, 2)
    even = 1 - lax.rem(l1, 2)
    r_base = SIB_STEPS
    s_base = r_base + depth * HOP_STEPS
    b_base = s_base + (l2 - 1) * HOP_STEPS

    def root(i):
        return depth - lax.rem(i, 2) * even

    def in_up_copy(i):
        return remote(1, i, x.at[i], in_up.at[i], me + s1)

    def in_dn_copy(i):
        return remote(2, i, x.at[i], in_dn.at[i], me - s1)

    def up_copy(i):
        return remote(3, i, up_s.at[i], up_r.at[i], me + s2)

    def dn_copy(i):
        return remote(4, i, dn_s.at[i], dn_r.at[i], me - s2)

    def share_copy(i):
        return remote(5, i, kvf.at[core, i], kvf.at[core, i], sibling)

    def out_up_copy(i):
        return remote(6, i, kvf.at[core, i], kvf.at[core, i], me + s1)

    def out_dn_copy(i):
        return remote(7, i, kvf.at[core, i], kvf.at[core, i], me - s1)

    def gather_in(t):
        iu = t - r_base - p1 * HOP_STEPS

        @pl.when(valid(iu))
        def _():
            @pl.when(p1 < root(iu))
            def _():
                @pl.when(p1 > 0)
                def _():
                    in_up_copy(iu).wait_recv()
                    x[iu] = x[iu] + in_up[iu]

                in_up_copy(iu).start()

        dn = t - r_base - (l1 - 1 - p1) * HOP_STEPS

        @pl.when(valid(dn))
        def _():
            @pl.when(p1 > root(dn))
            def _():
                @pl.when(p1 < l1 - 1)
                def _():
                    in_dn_copy(dn).wait_recv()
                    x[dn] = x[dn] + in_dn[dn]

                in_dn_copy(dn).start()

        ir = t - s_base

        @pl.when(valid(ir))
        def _():
            @pl.when(p1 == root(ir))
            def _():
                @pl.when(p1 > 0)
                def _():
                    in_up_copy(ir).wait_recv()
                    x[ir] = x[ir] + in_up[ir]

                @pl.when(p1 < l1 - 1)
                def _():
                    in_dn_copy(ir).wait_recv()
                    x[ir] = x[ir] + in_dn[ir]

    def across(t):
        up = t - s_base - p2 * HOP_STEPS

        @pl.when(valid(up))
        def _():
            @pl.when(p1 == root(up))
            def _():
                @pl.when(p2 > 0)
                def _():
                    up_copy(up).wait_recv()

                @pl.when(p2 < l2 - 1)
                def _():
                    @pl.when(p2 > 0)
                    def _():
                        up_s[up] = x[up] + up_r[up]

                    @pl.when(p2 == 0)
                    def _():
                        up_s[up] = x[up]

                    up_copy(up).start()

        dn = t - s_base - (l2 - 1 - p2) * HOP_STEPS

        @pl.when(valid(dn))
        def _():
            @pl.when(p1 == root(dn))
            def _():
                @pl.when(p2 < l2 - 1)
                def _():
                    dn_copy(dn).wait_recv()

                @pl.when(p2 > 0)
                def _():
                    @pl.when(p2 < l2 - 1)
                    def _():
                        dn_s[dn] = x[dn] + dn_r[dn]

                    @pl.when(p2 == l2 - 1)
                    def _():
                        dn_s[dn] = x[dn]

                    dn_copy(dn).start()

    def spread(t):
        end = t - b_base

        @pl.when(valid(end))
        def _():
            @pl.when(p1 == root(end))
            def _():
                @pl.when((p2 > 0) & (p2 < l2 - 1))
                def _():
                    kvf[core, end] = x[end] + up_r[end] + dn_r[end]

                @pl.when((p2 > 0) & (p2 == l2 - 1))
                def _():
                    kvf[core, end] = x[end] + up_r[end]

                @pl.when((p2 == 0) & (p2 < l2 - 1))
                def _():
                    kvf[core, end] = x[end] + dn_r[end]

                @pl.when(l2 == 1)
                def _():
                    kvf[core, end] = x[end]

                @pl.when(p1 < l1 - 1)
                def _():
                    out_up_copy(end).start()

                @pl.when(p1 > 0)
                def _():
                    out_dn_copy(end).start()

                share_copy(end).start()

        for back in (0, 1):
            above = p1 - (depth - back)
            i = t - b_base - jnp.where(above > 0, above, -above) * HOP_STEPS

            @pl.when(valid(i) & (above != 0))
            def _():
                @pl.when(root(i) == depth - back)
                def _():
                    @pl.when(above > 0)
                    def _():
                        out_up_copy(i).wait_recv()

                        @pl.when(p1 < l1 - 1)
                        def _():
                            out_up_copy(i).start()

                    @pl.when(above < 0)
                    def _():
                        out_dn_copy(i).wait_recv()

                        @pl.when(p1 > 0)
                        def _():
                            out_dn_copy(i).start()

                    share_copy(i).start()

    live = lax.broadcasted_iota(jnp.int32, (rows, HD), 0) < length
    batches = group // HEADS_AT_ONCE
    score_scale = 1.4426950408889634 / HD**0.5
    wide = HEADS_AT_ONCE * HD

    def result_copy(m):
        columns = pl.ds(pl.multiple_of(m * wide, wide), wide)
        return pltpu.make_async_copy(out_ref.at[:, columns], out_hbm.at[:, columns], out_sems.at[m])

    all_rows = pieces * (blk + pre)

    def attend(m):
        g, part = lax.div(m, batches), lax.rem(m, batches)
        first = g * group + part * HEADS_AT_ONCE
        keys = kvf[0, pl.ds(g * pieces, pieces)].reshape(all_rows, HD)
        values = kvf[1, pl.ds(g * pieces, pieces)].reshape(all_rows, HD)
        dims = (((1,), (1,)), ((), ()))
        v_far = jnp.concatenate([values, jnp.ones_like(values)], axis=1)
        own_k, own_v = nk_ref[:, cols(g)], nv_ref[:, cols(g)]
        v_own = jnp.concatenate([own_v, jnp.ones_like(own_v)], axis=1)
        mask = jnp.concatenate([bias[...]] * SUB, axis=0)
        for sub in range(0, HEADS_AT_ONCE, SUB):
            q = jnp.concatenate([q_ref[:, cols(first + sub + j)] for j in range(SUB)], axis=0)
            s_far = lax.dot_general(q, keys, dims, preferred_element_type=jnp.float32)
            s_own = lax.dot_general(q, own_k, dims, preferred_element_type=jnp.float32) + mask
            top = jnp.maximum(jnp.max(s_far, axis=1, keepdims=True), jnp.max(s_own, axis=1, keepdims=True))
            w_far = jnp.exp2((s_far - top) * score_scale).astype(jnp.bfloat16)
            w_own = jnp.exp2((s_own - top) * score_scale).astype(jnp.bfloat16)
            summed = jnp.dot(w_far, v_far, preferred_element_type=jnp.float32)
            summed += jnp.dot(w_own, v_own, preferred_element_type=jnp.float32)
            result = summed[:, :HD] / summed[:, HD:]
            for j in range(SUB):
                piece = jnp.where(live, result[j * rows : (j + 1) * rows], 0.0)
                out_ref[:, cols(first + sub + j)] = piece.astype(out_ref.dtype)

    hops = max(2 * (short // 2) + long - 1, 2 * (long // 2) + short - 1)
    c_base = SIB_STEPS + hops * HOP_STEPS + SIB_STEPS
    attends = kv_heads * batches
    per = max(pieces // batches, 1)
    steps = c_base + max(chunks, pieces + (attends - 1) * per)

    def one_step(t, carry):
        @pl.when(t < chunks)
        def _():
            build(t)
            remote(0, t, sib_s.at[t], sib_r.at[t], sibling).start()

        i = t - r_base

        @pl.when(valid(i))
        def _():
            remote(0, i, sib_s.at[i], sib_r.at[i], sibling).wait_recv()
            x[i] = x[i] + sib_r[i]

        gather_in(t)
        across(t)
        spread(t)
        i_c = t - c_base

        @pl.when(valid(i_c))
        def _():
            remote(5, i_c, kvf.at[core, i_c], kvf.at[1 - core, i_c], sibling).wait_recv()

        late = t - c_base - (pieces - 1)

        @pl.when(late == 0)
        def _():
            q_copy.wait()

        @pl.when((late >= 0) & (late < attends * per) & (lax.rem(late, per) == 0))
        def _():
            m = lax.div(late, per)
            attend(m)
            result_copy(m).start()

        return carry

    lax.fori_loop(0, steps, one_step, 0)

    def drain(i, carry):
        remote(0, i, sib_s.at[i], sib_r.at[i], sibling).wait_send()
        share_copy(i).wait_send()
        at = root(i)
        for used, copy in (
            (p1 < at, in_up_copy),
            (p1 > at, in_dn_copy),
            ((p1 == at) & (p2 < l2 - 1), up_copy),
            ((p1 == at) & (p2 > 0), dn_copy),
            ((p1 >= at) & (p1 < l1 - 1), out_up_copy),
            ((p1 <= at) & (p1 > 0), out_dn_copy),
        ):
            @pl.when(used)
            def _():
                copy(i).wait_send()

        return carry

    lax.fori_loop(0, chunks, drain, 0)

    def drain_result(m, carry):
        result_copy(m).wait()
        return carry

    lax.fori_loop(0, attends, drain_result, 0)


def solution(mesh):
    ring = mesh.shape["ctx"]

    def body(queries, new_keys, new_values, prefix_keys, prefix_values, pool_keys, pool_values, owners, lengths):
        heads = queries.shape[1] // HD
        kv_heads = new_keys.shape[1] // HD
        pieces = pool_keys.shape[1] * CUTS
        chunks = kv_heads * pieces
        c_rows = pool_keys.shape[2] // CUTS + prefix_keys.shape[0] * ring // pieces
        chunk_buf = pltpu.VMEM((chunks, c_rows, HD), jnp.bfloat16)
        vm = pl.BlockSpec(memory_space=pltpu.VMEM)
        hbm = pl.BlockSpec(memory_space=pl.ANY)
        sm = pl.BlockSpec(memory_space=pltpu.SMEM)
        return pl.pallas_call(
            functools.partial(kernel, ring, heads, kv_heads),
            out_shape=jax.ShapeDtypeStruct(queries.shape, jnp.bfloat16),
            in_specs=[hbm] + [vm] * 6 + [sm] * 2,
            out_specs=hbm,
            scratch_shapes=[chunk_buf] * 9
            + [
                pltpu.VMEM((2, chunks, c_rows, HD), jnp.bfloat16),
                pltpu.VMEM((queries.shape[0], queries.shape[0]), jnp.float32),
                pltpu.VMEM(queries.shape, jnp.bfloat16),
                pltpu.VMEM(queries.shape, jnp.bfloat16),
                pltpu.SemaphoreType.DMA((8, chunks)),
                pltpu.SemaphoreType.DMA((8, chunks)),
                pltpu.SemaphoreType.DMA,
                pltpu.SemaphoreType.DMA((heads // HEADS_AT_ONCE,)),
            ],
            compiler_params=pltpu.CompilerParams(
                collective_id=0, has_side_effects=True, vmem_limit_bytes=67043328
            ),
        )(queries, new_keys, new_values, prefix_keys, prefix_values, pool_keys, pool_values, owners, lengths)

    two = P(("groups", "ctx"), None)
    four = P(("groups", "ctx"), None, None, None)
    return jax.shard_map(
        body, mesh=mesh, in_specs=(two,) * 5 + (four,) * 2 + (P("groups"), P(("groups", "ctx"))),
        out_specs=two, check_vma=False,
    )
```

profile of v0, /device:TPU:0, one launch (start us, length us, event | category | flops | bytes accessed | tf_op | source)
XLA Modules:
  0.0 54.8 jit_solution(17648590070841496743)
XLA Ops:
  0.7 51.0 %shard_map.91 = bf16[128,8192]{1,0:T(8,128)(2,1)} custom-call(bf16[128,8192]{1,0:T(8,128)(2,1)} %q_hbm.1, bf16[128,1024]{1,0:T(8,128)(2,1)} %nk_ref.1, bf16[128,1024]{1,0:T(8,128)(2,1)} %nv_ref.1, bf16[8,1024]{1,0:T(8,128)(2,1)} %pk_ref.1, bf16[8,1024]{1,0:T(8,128)(2,1)} %pv_ref.1, bf16[1,2,256,1024]{3,2,1,0:T(8,128)(2,1)} %poolk_ref.1, ...), custom_call_target="tpu_custom_call" | custom-call | tf_op jit(solution)/shard_map/pallas_call | solution.py:416
  51.7 3.1 %copy.12 = bf16[128,8192]{1,0:T(8,128)(2,1)} copy(bf16[128,8192]{1,0:T(8,128)(2,1)} %shard_map.91) | data formatting | bytes 4194304
where the time goes:
time: 55 us; the launch traced here: 54.8 us
  Pallas kernels  51 us (93%)
  local copies, waits for them, and re-layouts  3.1 us (6%)
  between operations  0.66 us (1%)
    pallas_call x1, Pallas kernels, body(): pl.pallas_call(functools.partial(kernel, ring, heads, kv_heads), out_shap...  51 us
    unnamed x1, local copies, waits for them, and re-layouts  3.1 us

commit v1 on v0

v1 whole, which is shorter than its diff:
```python
import functools

import jax
import jax.numpy as jnp
from jax import lax
from jax.experimental import pallas as pl
from jax.experimental.pallas import tpu as pltpu
from jax.sharding import PartitionSpec as P

HD = 128
CUTS = 1
SIB = 1
HOP = (5, 2)
SUB = 4


def grid_of(ring):
    chips = ring // 2
    short = 1
    while (short * 2) ** 2 <= chips and chips % (short * 2) == 0:
        short *= 2
    return chips // short, short


def kernel(
    ring, heads, kv_heads,
    q_hbm, nk_hbm, nv_hbm, pk_hbm, pv_hbm, poolk_hbm, poolv_hbm, owners_ref, lengths_ref,
    out_hbm,
    page, pre_in, x, sib_s, sib_r, in_up, in_dn, up_s, up_r, dn_s, dn_r, kvf, bias, q_ref, nk_ref, nv_ref, out_ref,
    page_sems, pre_sems, load_sems, send_sems, recv_sems, out_sems,
):
    long, short = grid_of(ring)
    me = lax.axis_index("ctx")
    core = lax.rem(me, 2)
    chip = lax.div(me, 2)
    py = lax.rem(chip, short)
    pz = lax.div(chip, short)
    sibling = me + 1 - 2 * core
    sy, sz = 2, 2 * short

    barrier = pltpu.get_barrier_semaphore()

    def greet(target):
        pl.semaphore_signal(barrier, inc=1, device_id={"ctx": target})

    greet(sibling)
    peers = 1
    for pos, size, step in ((py, short, sy), (pz, long, sz)):
        @pl.when(pos > 0)
        def _():
            greet(me - step)

        @pl.when(pos < size - 1)
        def _():
            greet(me + step)

        peers = peers + jnp.where(pos > 0, 1, 0) + jnp.where(pos < size - 1, 1, 0)

    pages = poolk_hbm.shape[1]
    pieces = pages * CUTS
    page_rows = poolk_hbm.shape[2]
    blk = page_rows // CUTS
    chunks = kv_heads * pieces
    pairs = chunks // 2
    per_head = pieces // 2
    own_rows = pk_hbm.shape[0]
    pre = own_rows * ring // pieces
    rows = q_hbm.shape[0]
    group = heads // kv_heads
    width = kv_heads * HD

    splits = ((0, HD), (HD, width - HD))

    def page_copy(src, slot, part):
        start, size = splits[part]
        return pltpu.make_async_copy(
            src.at[0, :, :, pl.ds(start, size)], page.at[slot, :, :, pl.ds(start, size)], page_sems.at[slot, part]
        )

    def pre_copy(src, slot):
        return pltpu.make_async_copy(src, pre_in.at[slot], pre_sems.at[slot])

    def fetch(k_slot):
        pre_copy(pk_hbm, k_slot).start()
        pre_copy(pv_hbm, 1 - k_slot).start()
        for part in range(2):
            page_copy(poolk_hbm, k_slot, part).start()
            page_copy(poolv_hbm, 1 - k_slot, part).start()

    @pl.when(core == 0)
    def _():
        fetch(0)

    @pl.when(core == 1)
    def _():
        fetch(1)

    loads = [
        pltpu.make_async_copy(src, dst, load_sems.at[n])
        for n, (src, dst) in enumerate(((q_hbm, q_ref), (nk_hbm, nk_ref), (nv_hbm, nv_ref)))
    ]
    for load in loads:
        load.start()

    length = lengths_ref[0]
    tok = lax.broadcasted_iota(jnp.int32, (rows, rows), 0)
    key = lax.broadcasted_iota(jnp.int32, (rows, rows), 1)
    bias[...] = jnp.where((key <= tok) & (key < length), 0.0, -1e30)

    def wait_pages(part):
        for slot in range(2):
            page_copy(poolk_hbm, slot, part).wait()

    for slot in range(2):
        pre_copy(pk_hbm, slot).wait()
    wait_pages(0)
    pl.semaphore_wait(barrier, peers)

    def remote(kind, b, i, src, dst, target):
        return pltpu.make_async_remote_copy(
            src_ref=src, dst_ref=dst, send_sem=send_sems.at[kind, b], recv_sem=recv_sems.at[kind, i],
            device_id={"ctx": target}, device_id_type=pl.DeviceIdType.MESH,
        )

    def cols(g):
        return pl.ds(pl.multiple_of(g * HD, HD), HD)

    def build(i):
        g, b = lax.div(i, pieces), lax.rem(i, pieces)
        page_of = lax.div(b, CUTS)
        start = pl.multiple_of(lax.rem(b, CUTS) * blk, blk)
        mine = jnp.where(owners_ref[page_of] == me, 1.0, 0.0).astype(jnp.float32)
        row = lax.broadcasted_iota(jnp.int32, (pre, HD), 0) + b * pre
        in_mine = (row >= me * own_rows) & (row < (me + 1) * own_rows)
        for slot, dst in ((1, sib_s), (0, x)):
            part = page[slot, page_of, pl.ds(start, blk), cols(g)]
            dst[i, :blk] = part * jnp.full(part.shape, mine, jnp.float32).astype(jnp.bfloat16)
            mine_pre = pre_in[slot, :, cols(g)].astype(jnp.float32)
            tiled = jnp.concatenate([mine_pre] * (pre // own_rows), axis=0)
            dst[i, blk:] = jnp.where(in_mine, tiled, 0.0).astype(jnp.bfloat16)

    def pair(u):
        return pl.ds(2 * u, 2)

    def sib_copy(u):
        return remote(0, 0, u, sib_s.at[pair(u)], sib_r.at[pair(u)], sibling)

    def in_up_copy(b, i):
        return remote(1, b, i, x.at[i], in_up.at[i], me + sy)

    def in_dn_copy(b, i):
        return remote(2, b, i, x.at[i], in_dn.at[i], me - sy)

    def up_copy(b, i, src):
        return remote(3, b, i, src.at[i], up_r.at[i], me + sz)

    def dn_copy(b, i, src):
        return remote(4, b, i, src.at[i], dn_r.at[i], me - sz)

    def share_copy(b, i):
        return remote(5, b, i, kvf.at[core, i], kvf.at[core, i], sibling)

    def out_up_copy(b, i):
        return remote(6, b, i, kvf.at[core, i], kvf.at[core, i], me + sy)

    def out_dn_copy(b, i):
        return remote(7, b, i, kvf.at[core, i], kvf.at[core, i], me - sy)

    depth = short // 2
    roots = (depth, depth - 1 + short % 2)

    def after(hops):
        return SIB + lax.div(hops * HOP[0], HOP[1]) if not isinstance(hops, int) else SIB + hops * HOP[0] // HOP[1]

    def at(u):
        return (u >= 0) & (u < pairs)

    def gather(t):
        u = t - SIB

        @pl.when(at(u))
        def _():
            sib_copy(u).wait_recv()
            x[pair(u)] = x[pair(u)] + sib_r[pair(u)]
            for b, root in enumerate(roots):
                if root > 0:
                    @pl.when(py == 0)
                    def _():
                        in_up_copy(b, 2 * u + b).start()

                if root < short - 1:
                    @pl.when(py == short - 1)
                    def _():
                        in_dn_copy(b, 2 * u + b).start()

        for b, root in enumerate(roots):
            for hop in range(1, root):
                up = t - after(hop)

                @pl.when(at(up) & (py == hop))
                def _():
                    i = 2 * up + b
                    in_up_copy(b, i).wait_recv()
                    x[i] = x[i] + in_up[i]
                    in_up_copy(b, i).start()

            for hop in range(1, short - 1 - root):
                dn = t - after(hop)

                @pl.when(at(dn) & (py == short - 1 - hop))
                def _():
                    i = 2 * dn + b
                    in_dn_copy(b, i).wait_recv()
                    x[i] = x[i] + in_dn[i]
                    in_dn_copy(b, i).start()

    def root_hops(root):
        return max(root, short - 1 - root)

    def scan(t):
        for b, root in enumerate(roots):
            hops = root_hops(root)
            r = t - after(hops)

            @pl.when(at(r) & (py == root))
            def _():
                i = 2 * r + b
                if root > 0:
                    in_up_copy(b, i).wait_recv()
                    x[i] = x[i] + in_up[i]
                if root < short - 1:
                    in_dn_copy(b, i).wait_recv()
                    x[i] = x[i] + in_dn[i]

                if long > 1:
                    @pl.when(pz == 0)
                    def _():
                        up_copy(b, i, x).start()

                    @pl.when(pz == long - 1)
                    def _():
                        dn_copy(b, i, x).start()

            up = t - after(hops + pz)

            @pl.when(at(up) & (py == root) & (pz > 0))
            def _():
                i = 2 * up + b
                up_copy(b, i, up_s).wait_recv()

                @pl.when(pz < long - 1)
                def _():
                    up_s[i] = x[i] + up_r[i]
                    up_copy(b, i, up_s).start()

            dn = t - after(hops + long - 1 - pz)

            @pl.when(at(dn) & (py == root) & (pz < long - 1))
            def _():
                i = 2 * dn + b
                dn_copy(b, i, dn_s).wait_recv()

                @pl.when(pz > 0)
                def _():
                    dn_s[i] = x[i] + dn_r[i]
                    dn_copy(b, i, dn_s).start()

    z_hops = jnp.maximum(pz, long - 1 - pz)

    def spread(t):
        for b, root in enumerate(roots):
            hops = root_hops(root) + z_hops
            end = t - after(hops)

            @pl.when(at(end) & (py == root))
            def _():
                i = 2 * end + b

                if long == 1:
                    kvf[core, i] = x[i]
                else:
                    @pl.when((pz > 0) & (pz < long - 1))
                    def _():
                        kvf[core, i] = x[i] + up_r[i] + dn_r[i]

                    @pl.when(pz == long - 1)
                    def _():
                        kvf[core, i] = x[i] + up_r[i]

                    @pl.when(pz == 0)
                    def _():
                        kvf[core, i] = x[i] + dn_r[i]

                if root < short - 1:
                    out_up_copy(b, i).start()
                if root > 0:
                    out_dn_copy(b, i).start()
                share_copy(b, i).start()

            above = jnp.where(py > root, py - root, root - py)
            out = t - after(hops + above)

            @pl.when(at(out) & (py > root))
            def _():
                i = 2 * out + b
                out_up_copy(b, i).wait_recv()

                @pl.when(py < short - 1)
                def _():
                    out_up_copy(b, i).start()

                share_copy(b, i).start()

            @pl.when(at(out) & (py < root))
            def _():
                i = 2 * out + b
                out_dn_copy(b, i).wait_recv()

                @pl.when(py > 0)
                def _():
                    out_dn_copy(b, i).start()

                share_copy(b, i).start()

    def far(root):
        return jnp.where(py > root, py - root, root - py)

    def arrive(t):
        for b, root in enumerate(roots):
            c = t - SIB - after(root_hops(root) + z_hops + far(root))

            @pl.when(at(c))
            def _():
                i = 2 * c + b
                remote(5, b, i, kvf.at[core, i], kvf.at[1 - core, i], sibling).wait_recv()

    live = lax.broadcasted_iota(jnp.int32, (rows, HD), 0) < length
    score_scale = 1.4426950408889634 / HD**0.5
    wide = group * HD

    def result_copy(g):
        columns = pl.ds(pl.multiple_of(g * wide, wide), wide)
        return pltpu.make_async_copy(out_ref.at[:, columns], out_hbm.at[:, columns], out_sems.at[g])

    all_rows = pieces * (blk + pre)

    def attend(g):
        first = g * group
        keys = kvf[0, pl.ds(g * pieces, pieces)].reshape(all_rows, HD)
        values = kvf[1, pl.ds(g * pieces, pieces)].reshape(all_rows, HD)
        dims = (((1,), (1,)), ((), ()))
        v_far = jnp.concatenate([values, jnp.ones_like(values)], axis=1)
        own_k, own_v = nk_ref[:, cols(g)], nv_ref[:, cols(g)]
        v_own = jnp.concatenate([own_v, jnp.ones_like(own_v)], axis=1)
        mask = jnp.concatenate([bias[...]] * SUB, axis=0)
        for sub in range(0, group, SUB):
            q = jnp.concatenate([q_ref[:, cols(first + sub + j)] for j in range(SUB)], axis=0)
            s_far = lax.dot_general(q, keys, dims, preferred_element_type=jnp.float32)
            s_own = lax.dot_general(q, own_k, dims, preferred_element_type=jnp.float32) + mask
            top = jnp.maximum(jnp.max(s_far, axis=1, keepdims=True), jnp.max(s_own, axis=1, keepdims=True))
            w_far = jnp.exp2((s_far - top) * score_scale).astype(jnp.bfloat16)
            w_own = jnp.exp2((s_own - top) * score_scale).astype(jnp.bfloat16)
            summed = jnp.dot(w_far, v_far, preferred_element_type=jnp.float32)
            summed += jnp.dot(w_own, v_own, preferred_element_type=jnp.float32)
            result = summed[:, :HD] / summed[:, HD:]
            for j in range(SUB):
                piece = jnp.where(live, result[j * rows : (j + 1) * rows], 0.0)
                out_ref[:, cols(first + sub + j)] = piece.astype(out_ref.dtype)

    reach = max(root_hops(root) + max(root, short - 1 - root) for root in roots)
    done = SIB + after(reach + z_hops)
    steps = SIB + after(reach + long - 1) + pairs

    def one_step(t, carry):
        @pl.when(t == 1)
        def _():
            wait_pages(1)

        @pl.when(t < pairs)
        def _():
            build(2 * t)
            build(2 * t + 1)
            sib_copy(t).start()

        gather(t)
        scan(t)
        spread(t)
        arrive(t)

        @pl.when(t == SIB + 1)
        def _():
            for load in loads:
                load.wait()

        u = t - done

        @pl.when(at(u) & (lax.rem(u, per_head) == per_head - 1))
        def _():
            g = lax.div(u, per_head)
            attend(g)
            result_copy(g).start()

        return carry

    lax.fori_loop(0, steps, one_step, 0)

    half = pl.ds(0, pairs)
    every = pl.ds(0, chunks)
    remote(0, 0, 0, sib_s.at[every], sib_r.at[every], sibling).wait_send()
    for b, root in enumerate(roots):
        for kind, used in (
            (1, py < root),
            (2, py > root),
            (3, (py == root) & (pz < long - 1)),
            (4, (py == root) & (pz > 0)),
            (5, py >= 0),
            (6, (py >= root) & (py < short - 1)),
            (7, (py <= root) & (py > 0)),
        ):
            @pl.when(used)
            def _():
                remote(kind, b, 0, x.at[half], sib_r.at[half], sibling).wait_send()

    for g in range(kv_heads):
        result_copy(g).wait()


def solution(mesh):
    ring = mesh.shape["ctx"]

    def body(queries, new_keys, new_values, prefix_keys, prefix_values, pool_keys, pool_values, owners, lengths):
        heads = queries.shape[1] // HD
        kv_heads = new_keys.shape[1] // HD
        pages, page_rows = pool_keys.shape[1:3]
        pieces = pages * CUTS
        chunks = kv_heads * pieces
        c_rows = page_rows // CUTS + prefix_keys.shape[0] * ring // pieces
        chunk_buf = pltpu.VMEM((chunks, c_rows, HD), jnp.bfloat16)
        hbm = pl.BlockSpec(memory_space=pl.ANY)
        sm = pl.BlockSpec(memory_space=pltpu.SMEM)
        return pl.pallas_call(
            functools.partial(kernel, ring, heads, kv_heads),
            out_shape=jax.ShapeDtypeStruct(queries.shape, jnp.bfloat16),
            in_specs=[hbm] * 7 + [sm] * 2,
            out_specs=hbm,
            scratch_shapes=[
                pltpu.VMEM((2, pages, page_rows, kv_heads * HD), jnp.bfloat16),
                pltpu.VMEM((2,) + prefix_keys.shape, jnp.bfloat16),
            ]
            + [chunk_buf] * 9
            + [
                pltpu.VMEM((2, chunks, c_rows, HD), jnp.bfloat16),
                pltpu.VMEM((queries.shape[0], queries.shape[0]), jnp.float32),
                pltpu.VMEM(queries.shape, jnp.bfloat16),
                pltpu.VMEM(new_keys.shape, jnp.bfloat16),
                pltpu.VMEM(new_values.shape, jnp.bfloat16),
                pltpu.VMEM(queries.shape, jnp.bfloat16),
                pltpu.SemaphoreType.DMA((2, 2)),
                pltpu.SemaphoreType.DMA((2,)),
                pltpu.SemaphoreType.DMA((3,)),
                pltpu.SemaphoreType.DMA((8, 2)),
                pltpu.SemaphoreType.DMA((8, chunks)),
                pltpu.SemaphoreType.DMA((kv_heads,)),
            ],
            compiler_params=pltpu.CompilerParams(
                collective_id=0, has_side_effects=True, vmem_limit_bytes=67043328
            ),
        )(queries, new_keys, new_values, prefix_keys, prefix_values, pool_keys, pool_values, owners, lengths)

    two = P(("groups", "ctx"), None)
    four = P(("groups", "ctx"), None, None, None)
    return jax.shard_map(
        body, mesh=mesh, in_specs=(two,) * 5 + (four,) * 2 + (P("groups"), P(("groups", "ctx"))),
        out_specs=two, check_vma=False,
    )
```

time: 55 us -> 50.3 us (0.915)
  Pallas kernels: 51 us -> 46.4 us
    pallas_call x1, Pallas kernels: 51 us -> 46.4 us  [body(): pl.pallas_call(functools.partial(kernel, ring, heads, kv_heads), out_shap...]
where the time goes in v1:
time: 50.3 us; the launch traced here: 50.1 us
  Pallas kernels  46.4 us (92%)
  local copies, waits for them, and re-layouts  3.1 us (6%)
  between operations  0.66 us (1%)
    pallas_call x1, Pallas kernels, body(): pl.pallas_call(functools.partial(kernel, ring, heads, kv_heads), out_shap...  46.4 us
    unnamed x1, local copies, waits for them, and re-layouts  3.1 us

profile of v1, /device:TPU:0, one launch (start us, length us, event | category | flops | bytes accessed | tf_op | source)
XLA Modules:
  0.0 50.1 jit_solution(11184619147054666740)
XLA Ops:
  0.7 46.4 %shard_map.91 = bf16[128,8192]{1,0:T(8,128)(2,1)} custom-call(bf16[128,8192]{1,0:T(8,128)(2,1)} %q_hbm.1, bf16[128,1024]{1,0:T(8,128)(2,1)} %nk_hbm.1, bf16[128,1024]{1,0:T(8,128)(2,1)} %nv_hbm.1, bf16[8,1024]{1,0:T(8,128)(2,1)} %pk_hbm.1, bf16[8,1024]{1,0:T(8,128)(2,1)} %pv_hbm.1, bf16[1,2,256,1024]{3,2,1,0:T(8,128)(2,1)} %poolk_hbm.1, ...), custom_call_target="tpu_custom_call" | custom-call | tf_op jit(solution)/shard_map/pallas_call | solution.py:441
  47.0 3.1 %copy.12 = bf16[128,8192]{1,0:T(8,128)(2,1)} copy(bf16[128,8192]{1,0:T(8,128)(2,1)} %shard_map.91) | data formatting | bytes 4194304

commit v2 on v1

--- a/solution.py
+++ b/solution.py
@@ -10,8 +10,10 @@
 HD = 128
 CUTS = 1
 SIB = 1
-HOP = (5, 2)
+HOP = (3, 1)
 SUB = 4
+PRE_STEPS = (2, 5, 6)
+NEAR_STEP = 7
 
 
 def grid_of(ring):
@@ -26,8 +28,8 @@
     ring, heads, kv_heads,
     q_hbm, nk_hbm, nv_hbm, pk_hbm, pv_hbm, poolk_hbm, poolv_hbm, owners_ref, lengths_ref,
     out_hbm,
-    page, pre_in, x, sib_s, sib_r, in_up, in_dn, up_s, up_r, dn_s, dn_r, kvf, bias, q_ref, nk_ref, nv_ref, out_ref,
-    page_sems, pre_sems, load_sems, send_sems, recv_sems, out_sems,
+    page, pref, x, sib_s, sib_r, in_up, in_dn, up_s, up_r, dn_s, dn_r, kvf, bias, q_ref, nk_ref, nv_ref, out_ref, near_sum, near_top,
+    page_sems, load_sems, pre_send, pre_recv, send_sems, recv_sems, out_sems,
 ):
     long, short = grid_of(ring)
     me = lax.axis_index("ctx")
@@ -43,18 +45,18 @@
     def greet(target):
         pl.semaphore_signal(barrier, inc=1, device_id={"ctx": target})
 
+    def y_peer(d):
+        return me + (lax.rem(py + d, short) - py) * sy
+
+    def z_peer(d):
+        return me + (lax.rem(pz + d, long) - pz) * sz
+
     greet(sibling)
-    peers = 1
-    for pos, size, step in ((py, short, sy), (pz, long, sz)):
-        @pl.when(pos > 0)
-        def _():
-            greet(me - step)
-
-        @pl.when(pos < size - 1)
-        def _():
-            greet(me + step)
-
-        peers = peers + jnp.where(pos > 0, 1, 0) + jnp.where(pos < size - 1, 1, 0)
+    for d in range(1, short):
+        greet(y_peer(d))
+    for d in range(1, long):
+        greet(z_peer(d))
+    peers = 1 + short - 1 + long - 1
 
     pages = poolk_hbm.shape[1]
     pieces = pages * CUTS
@@ -64,7 +66,7 @@
     pairs = chunks // 2
     per_head = pieces // 2
     own_rows = pk_hbm.shape[0]
-    pre = own_rows * ring // pieces
+    pre = own_rows * ring
     rows = q_hbm.shape[0]
     group = heads // kv_heads
     width = kv_heads * HD
@@ -77,12 +79,7 @@
             src.at[0, :, :, pl.ds(start, size)], page.at[slot, :, :, pl.ds(start, size)], page_sems.at[slot, part]
         )
 
-    def pre_copy(src, slot):
-        return pltpu.make_async_copy(src, pre_in.at[slot], pre_sems.at[slot])
-
     def fetch(k_slot):
-        pre_copy(pk_hbm, k_slot).start()
-        pre_copy(pv_hbm, 1 - k_slot).start()
         for part in range(2):
             page_copy(poolk_hbm, k_slot, part).start()
             page_copy(poolv_hbm, 1 - k_slot, part).start()
@@ -95,9 +92,14 @@
     def _():
         fetch(1)
 
+    mine = pref.at[core, pz, py]
+    own_pre = [pltpu.make_async_copy(src, mine.at[n], load_sems.at[n]) for n, src in enumerate((pk_hbm, pv_hbm))]
+    for load in own_pre:
+        load.start()
+
     loads = [
         pltpu.make_async_copy(src, dst, load_sems.at[n])
-        for n, (src, dst) in enumerate(((q_hbm, q_ref), (nk_hbm, nk_ref), (nv_hbm, nv_ref)))
+        for n, (src, dst) in enumerate(((q_hbm, q_ref), (nk_hbm, nk_ref), (nv_hbm, nv_ref)), start=2)
     ]
     for load in loads:
         load.start()
@@ -111,10 +113,50 @@
         for slot in range(2):
             page_copy(poolk_hbm, slot, part).wait()
 
-    for slot in range(2):
-        pre_copy(pk_hbm, slot).wait()
+    def pre_y(d, source):
+        return pltpu.make_async_remote_copy(
+            src_ref=mine, dst_ref=mine, send_sem=pre_send.at[source], recv_sem=pre_recv.at[source],
+            device_id={"ctx": y_peer(d)}, device_id_type=pl.DeviceIdType.MESH,
+        )
+
+    def pre_z(d, source):
+        row = pref.at[core, pz]
+        return pltpu.make_async_remote_copy(
+            src_ref=row, dst_ref=row, send_sem=pre_send.at[short + source], recv_sem=pre_recv.at[short + source],
+            device_id={"ctx": z_peer(d)}, device_id_type=pl.DeviceIdType.MESH,
+        )
+
+    def pre_sib(slot):
+        return pltpu.make_async_remote_copy(
+            src_ref=pref.at[slot], dst_ref=pref.at[slot], send_sem=pre_send.at[short + long], recv_sem=pre_recv.at[short + long],
+            device_id={"ctx": sibling}, device_id_type=pl.DeviceIdType.MESH,
+        )
+
+    def pre_step(n):
+        if n == 0:
+            for d in range(1, short):
+                pltpu.make_async_remote_copy(
+                    src_ref=mine, dst_ref=pref.at[core, pz, lax.rem(py + short - d, short)], send_sem=pre_send.at[d],
+                    recv_sem=pre_recv.at[d], device_id={"ctx": y_peer(d)}, device_id_type=pl.DeviceIdType.MESH,
+                ).wait_recv()
+            for d in range(1, long):
+                pre_z(d, d).start()
+        elif n == 1:
+            for d in range(1, long):
+                pltpu.make_async_remote_copy(
+                    src_ref=pref.at[core, pz], dst_ref=pref.at[core, lax.rem(pz + long - d, long)], send_sem=pre_send.at[short + d],
+                    recv_sem=pre_recv.at[short + d], device_id={"ctx": z_peer(d)}, device_id_type=pl.DeviceIdType.MESH,
+                ).wait_recv()
+            pre_sib(core).start()
+        else:
+            pre_sib(1 - core).wait_recv()
+
+    for load in own_pre:
+        load.wait()
     wait_pages(0)
     pl.semaphore_wait(barrier, peers)
+    for d in range(1, short):
+        pre_y(d, d).start()
 
     def remote(kind, b, i, src, dst, target):
         return pltpu.make_async_remote_copy(
@@ -129,15 +171,10 @@
         g, b = lax.div(i, pieces), lax.rem(i, pieces)
         page_of = lax.div(b, CUTS)
         start = pl.multiple_of(lax.rem(b, CUTS) * blk, blk)
-        mine = jnp.where(owners_ref[page_of] == me, 1.0, 0.0).astype(jnp.float32)
-        row = lax.broadcasted_iota(jnp.int32, (pre, HD), 0) + b * pre
-        in_mine = (row >= me * own_rows) & (row < (me + 1) * own_rows)
+        held = jnp.where(owners_ref[page_of] == me, 1.0, 0.0).astype(jnp.float32)
         for slot, dst in ((1, sib_s), (0, x)):
             part = page[slot, page_of, pl.ds(start, blk), cols(g)]
-            dst[i, :blk] = part * jnp.full(part.shape, mine, jnp.float32).astype(jnp.bfloat16)
-            mine_pre = pre_in[slot, :, cols(g)].astype(jnp.float32)
-            tiled = jnp.concatenate([mine_pre] * (pre // own_rows), axis=0)
-            dst[i, blk:] = jnp.where(in_mine, tiled, 0.0).astype(jnp.bfloat16)
+            dst[i] = part * jnp.full(part.shape, held, jnp.float32).astype(jnp.bfloat16)
 
     def pair(u):
         return pl.ds(2 * u, 2)
@@ -342,30 +379,47 @@
         columns = pl.ds(pl.multiple_of(g * wide, wide), wide)
         return pltpu.make_async_copy(out_ref.at[:, columns], out_hbm.at[:, columns], out_sems.at[g])
 
-    all_rows = pieces * (blk + pre)
+    all_rows = pieces * blk
+
+    dims = (((1,), (1,)), ((), ()))
+
+    def with_ones(values):
+        return jnp.concatenate([values, jnp.ones_like(values)], axis=1)
+
+    def query_rows(head):
+        return jnp.concatenate([q_ref[:, cols(head + j)] for j in range(SUB)], axis=0)
+
+    def near(g):
+        keys = jnp.concatenate([pref[:, :, :, 0, :, cols(g)].reshape(pre, HD), nk_ref[:, cols(g)]], axis=0)
+        values = jnp.concatenate([pref[:, :, :, 1, :, cols(g)].reshape(pre, HD), nv_ref[:, cols(g)]], axis=0)
+        values = with_ones(values)
+        mask = jnp.concatenate([jnp.zeros((rows, pre), jnp.float32), bias[...]], axis=1)
+        mask = jnp.concatenate([mask] * SUB, axis=0)
+        for sub in range(0, group, SUB):
+            scores = lax.dot_general(query_rows(g * group + sub), keys, dims, preferred_element_type=jnp.float32) + mask
+            top = jnp.max(scores, axis=1, keepdims=True)
+            weights = jnp.exp2((scores - top) * score_scale).astype(jnp.bfloat16)
+            part = pl.ds(sub * rows, SUB * rows)
+            near_sum[g, part] = jnp.dot(weights, values, preferred_element_type=jnp.float32)
+            near_top[g, part] = jnp.broadcast_to(top, (SUB * rows, HD))
 
     def attend(g):
-        first = g * group
         keys = kvf[0, pl.ds(g * pieces, pieces)].reshape(all_rows, HD)
-        values = kvf[1, pl.ds(g * pieces, pieces)].reshape(all_rows, HD)
-        dims = (((1,), (1,)), ((), ()))
-        v_far = jnp.concatenate([values, jnp.ones_like(values)], axis=1)
-        own_k, own_v = nk_ref[:, cols(g)], nv_ref[:, cols(g)]
-        v_own = jnp.concatenate([own_v, jnp.ones_like(own_v)], axis=1)
-        mask = jnp.concatenate([bias[...]] * SUB, axis=0)
+        values = with_ones(kvf[1, pl.ds(g * pieces, pieces)].reshape(all_rows, HD))
         for sub in range(0, group, SUB):
-            q = jnp.concatenate([q_ref[:, cols(first + sub + j)] for j in range(SUB)], axis=0)
-            s_far = lax.dot_general(q, keys, dims, preferred_element_type=jnp.float32)
-            s_own = lax.dot_general(q, own_k, dims, preferred_element_type=jnp.float32) + mask
-            top = jnp.maximum(jnp.max(s_far, axis=1, keepdims=True), jnp.max(s_own, axis=1, keepdims=True))
-            w_far = jnp.exp2((s_far - top) * score_scale).astype(jnp.bfloat16)
-            w_own = jnp.exp2((s_own - top) * score_scale).astype(jnp.bfloat16)
-            summed = jnp.dot(w_far, v_far, preferred_element_type=jnp.float32)
-            summed += jnp.dot(w_own, v_own, preferred_element_type=jnp.float32)
+            scores = lax.dot_general(query_rows(g * group + sub), keys, dims, preferred_element_type=jnp.float32)
+            part = pl.ds(sub * rows, SUB * rows)
+            before = near_top[g, part]
+            top = jnp.maximum(jnp.max(scores, axis=1, keepdims=True), before)
+            wide_top = jnp.concatenate([top] * (all_rows // HD), axis=1)
+            weights = jnp.exp2((scores - wide_top) * score_scale).astype(jnp.bfloat16)
+            scale = jnp.exp2((before - top) * score_scale)
+            summed = jnp.dot(weights, values, preferred_element_type=jnp.float32)
+            summed += jnp.concatenate([scale, scale], axis=1) * near_sum[g, part]
             result = summed[:, :HD] / summed[:, HD:]
             for j in range(SUB):
                 piece = jnp.where(live, result[j * rows : (j + 1) * rows], 0.0)
-                out_ref[:, cols(first + sub + j)] = piece.astype(out_ref.dtype)
+                out_ref[:, cols(g * group + sub + j)] = piece.astype(out_ref.dtype)
 
     reach = max(root_hops(root) + max(root, short - 1 - root) for root in roots)
     done = SIB + after(reach + z_hops)
@@ -382,15 +436,26 @@
             build(2 * t + 1)
             sib_copy(t).start()
 
+        @pl.when(t == SIB + 1)
+        def _():
+            for load in loads:
+                load.wait()
+
+        ahead = t - NEAR_STEP
+
+        @pl.when((ahead >= 0) & (ahead < kv_heads))
+        def _():
+            near(ahead)
+
         gather(t)
         scan(t)
         spread(t)
         arrive(t)
 
-        @pl.when(t == SIB + 1)
-        def _():
-            for load in loads:
-                load.wait()
+        for n in range(3):
+            @pl.when(t == PRE_STEPS[n])
+            def _():
+                pre_step(n)
 
         u = t - done
 
@@ -404,6 +469,11 @@
 
     lax.fori_loop(0, steps, one_step, 0)
 
+    for d in range(1, short):
+        pre_y(d, d).wait_send()
+    for d in range(1, long):
+        pre_z(d, d).wait_send()
+    pre_sib(core).wait_send()
     half = pl.ds(0, pairs)
     every = pl.ds(0, chunks)
     remote(0, 0, 0, sib_s.at[every], sib_r.at[every], sibling).wait_send()
@@ -434,7 +504,8 @@
         pages, page_rows = pool_keys.shape[1:3]
         pieces = pages * CUTS
         chunks = kv_heads * pieces
-        c_rows = page_rows // CUTS + prefix_keys.shape[0] * ring // pieces
+        c_rows = page_rows // CUTS
+        long, short = grid_of(ring)
         chunk_buf = pltpu.VMEM((chunks, c_rows, HD), jnp.bfloat16)
         hbm = pl.BlockSpec(memory_space=pl.ANY)
         sm = pl.BlockSpec(memory_space=pltpu.SMEM)
@@ -445,7 +516,7 @@
             out_specs=hbm,
             scratch_shapes=[
                 pltpu.VMEM((2, pages, page_rows, kv_heads * HD), jnp.bfloat16),
-                pltpu.VMEM((2,) + prefix_keys.shape, jnp.bfloat16),
+                pltpu.VMEM((2, long, short, 2) + prefix_keys.shape, jnp.bfloat16),
             ]
             + [chunk_buf] * 9
             + [
@@ -455,9 +526,12 @@
                 pltpu.VMEM(new_keys.shape, jnp.bfloat16),
                 pltpu.VMEM(new_values.shape, jnp.bfloat16),
                 pltpu.VMEM(queries.shape, jnp.bfloat16),
+                pltpu.VMEM((kv_heads, queries.shape[0] * heads // kv_heads, 2 * HD), jnp.float32),
+                pltpu.VMEM((kv_heads, queries.shape[0] * heads // kv_heads, HD), jnp.float32),
                 pltpu.SemaphoreType.DMA((2, 2)),
-                pltpu.SemaphoreType.DMA((2,)),
-                pltpu.SemaphoreType.DMA((3,)),
+                pltpu.SemaphoreType.DMA((5,)),
+                pltpu.SemaphoreType.DMA((short + long + 1,)),
+                pltpu.SemaphoreType.DMA((short + long + 1,)),
                 pltpu.SemaphoreType.DMA((8, 2)),
                 pltpu.SemaphoreType.DMA((8, chunks)),
                 pltpu.SemaphoreType.DMA((kv_heads,)),

time: 50.3 us -> 46.7 us (0.928)
  Pallas kernels: 46.4 us -> 42.8 us
    pallas_call x1, Pallas kernels: 46.4 us -> 42.8 us  [body(): pl.pallas_call(functools.partial(kernel, ring, heads, kv_heads), out_shap...]
where the time goes in v2:
time: 46.7 us; the launch traced here: 46.6 us
  Pallas kernels  42.8 us (92%)
  local copies, waits for them, and re-layouts  3.1 us (7%)
  between operations  0.66 us (1%)
    pallas_call x1, Pallas kernels, body(): pl.pallas_call(functools.partial(kernel, ring, heads, kv_heads), out_shap...  42.8 us
    unnamed x1, local copies, waits for them, and re-layouts  3.1 us

profile of v2, /device:TPU:0, one launch (start us, length us, event | category | flops | bytes accessed | tf_op | source)
XLA Modules:
  0.0 46.6 jit_solution(15983981727004765638)
XLA Ops:
  0.7 42.8 %shard_map.91 = bf16[128,8192]{1,0:T(8,128)(2,1)} custom-call(bf16[128,8192]{1,0:T(8,128)(2,1)} %q_hbm.1, bf16[128,1024]{1,0:T(8,128)(2,1)} %nk_hbm.1, bf16[128,1024]{1,0:T(8,128)(2,1)} %nv_hbm.1, bf16[8,1024]{1,0:T(8,128)(2,1)} %pk_hbm.1, bf16[8,1024]{1,0:T(8,128)(2,1)} %pv_hbm.1, bf16[1,2,256,1024]{3,2,1,0:T(8,128)(2,1)} %poolk_hbm.1, ...), custom_call_target="tpu_custom_call" | custom-call | tf_op jit(solution)/shard_map/pallas_call | solution.py:512
  43.5 3.1 %copy.12 = bf16[128,8192]{1,0:T(8,128)(2,1)} copy(bf16[128,8192]{1,0:T(8,128)(2,1)} %shard_map.91) | data formatting | bytes 4194304

commit v3 on v2

--- a/solution.py
+++ b/solution.py
@@ -14,6 +14,7 @@
 SUB = 4
 PRE_STEPS = (2, 5, 6)
 NEAR_STEP = 7
+STORES = 4
 
 
 def grid_of(ring):
@@ -27,9 +28,9 @@
 def kernel(
     ring, heads, kv_heads,
     q_hbm, nk_hbm, nv_hbm, pk_hbm, pv_hbm, poolk_hbm, poolv_hbm, owners_ref, lengths_ref,
-    out_hbm,
-    page, pref, x, sib_s, sib_r, in_up, in_dn, up_s, up_r, dn_s, dn_r, kvf, bias, q_ref, nk_ref, nv_ref, out_ref, near_sum, near_top,
-    page_sems, load_sems, pre_send, pre_recv, send_sems, recv_sems, out_sems,
+    out_ref,
+    page, pref, x, sib_s, sib_r, in_up, in_dn, up_s, up_r, dn_s, dn_r, kvf, bias, q_ref, nk_ref, nv_ref, near_sum, near_top,
+    page_sems, load_sems, pre_send, pre_recv, send_sems, recv_sems,
 ):
     long, short = grid_of(ring)
     me = lax.axis_index("ctx")
@@ -373,12 +374,6 @@
 
     live = lax.broadcasted_iota(jnp.int32, (rows, HD), 0) < length
     score_scale = 1.4426950408889634 / HD**0.5
-    wide = group * HD
-
-    def result_copy(g):
-        columns = pl.ds(pl.multiple_of(g * wide, wide), wide)
-        return pltpu.make_async_copy(out_ref.at[:, columns], out_hbm.at[:, columns], out_sems.at[g])
-
     all_rows = pieces * blk
 
     dims = (((1,), (1,)), ((), ()))
@@ -463,7 +458,6 @@
         def _():
             g = lax.div(u, per_head)
             attend(g)
-            result_copy(g).start()
 
         return carry
 
@@ -491,8 +485,17 @@
             def _():
                 remote(kind, b, 0, x.at[half], sib_r.at[half], sibling).wait_send()
 
-    for g in range(kv_heads):
-        result_copy(g).wait()
+
+def store(held_ref, out_hbm, sems):
+    rows = held_ref.shape[0] // STORES
+    copies = [
+        pltpu.make_async_copy(held_ref.at[pl.ds(n * rows, rows)], out_hbm.at[pl.ds(n * rows, rows)], sems.at[n])
+        for n in range(STORES)
+    ]
+    for copy in copies:
+        copy.start()
+    for copy in copies:
+        copy.wait()
 
 
 def solution(mesh):
@@ -509,11 +512,12 @@
         chunk_buf = pltpu.VMEM((chunks, c_rows, HD), jnp.bfloat16)
         hbm = pl.BlockSpec(memory_space=pl.ANY)
         sm = pl.BlockSpec(memory_space=pltpu.SMEM)
-        return pl.pallas_call(
+        vmem = pl.BlockSpec(memory_space=pltpu.VMEM)
+        held = pl.pallas_call(
             functools.partial(kernel, ring, heads, kv_heads),
-            out_shape=jax.ShapeDtypeStruct(queries.shape, jnp.bfloat16),
+            out_shape=pltpu.VMEM(queries.shape, jnp.bfloat16),
             in_specs=[hbm] * 7 + [sm] * 2,
-            out_specs=hbm,
+            out_specs=vmem,
             scratch_shapes=[
                 pltpu.VMEM((2, pages, page_rows, kv_heads * HD), jnp.bfloat16),
                 pltpu.VMEM((2, long, short, 2) + prefix_keys.shape, jnp.bfloat16),
@@ -525,7 +529,6 @@
                 pltpu.VMEM(queries.shape, jnp.bfloat16),
                 pltpu.VMEM(new_keys.shape, jnp.bfloat16),
                 pltpu.VMEM(new_values.shape, jnp.bfloat16),
-                pltpu.VMEM(queries.shape, jnp.bfloat16),
                 pltpu.VMEM((kv_heads, queries.shape[0] * heads // kv_heads, 2 * HD), jnp.float32),
                 pltpu.VMEM((kv_heads, queries.shape[0] * heads // kv_heads, HD), jnp.float32),
                 pltpu.SemaphoreType.DMA((2, 2)),
@@ -534,12 +537,19 @@
                 pltpu.SemaphoreType.DMA((short + long + 1,)),
                 pltpu.SemaphoreType.DMA((8, 2)),
                 pltpu.SemaphoreType.DMA((8, chunks)),
-                pltpu.SemaphoreType.DMA((kv_heads,)),
             ],
             compiler_params=pltpu.CompilerParams(
-                collective_id=0, has_side_effects=True, vmem_limit_bytes=67043328
+                collective_id=0, has_side_effects=True, vmem_limit_bytes=56 * 2**20
             ),
         )(queries, new_keys, new_values, prefix_keys, prefix_values, pool_keys, pool_values, owners, lengths)
+        return pl.pallas_call(
+            store,
+            out_shape=jax.ShapeDtypeStruct(queries.shape, jnp.bfloat16),
+            in_specs=[vmem],
+            out_specs=hbm,
+            scratch_shapes=[pltpu.SemaphoreType.DMA((STORES,))],
+            compiler_params=pltpu.CompilerParams(vmem_limit_bytes=2**20),
+        )(held)
 
     two = P(("groups", "ctx"), None)
     four = P(("groups", "ctx"), None, None, None)

time: 46.7 us -> 44.2 us (0.946)
  local copies, waits for them, and re-layouts: 3.1 us -> 0 us
  Pallas kernels: 42.8 us -> 43.4 us
    unnamed x1 -> x0, local copies, waits for them, and re-layouts: 3.1 us -> none
    pallas_call x0 -> x1, Pallas kernels: none -> 1.35 us  [body(): pl.pallas_call(store, out_shape=jax.ShapeDtypeStruct(queries.shape, jnp.b...]
    pallas_call x1, Pallas kernels: 42.8 us -> 42 us  [body(): pl.pallas_call(functools.partial(kernel, ring, heads, kv_heads), out_shap...]
where the time goes in v3:
time: 44.2 us; the launch traced here: 44 us
  Pallas kernels  43.4 us (98%)
  between operations  0.66 us (1%)
    pallas_call x1, Pallas kernels, body(): pl.pallas_call(functools.partial(kernel, ring, heads, kv_heads), out_shap...  42 us
    pallas_call x1, Pallas kernels, body(): pl.pallas_call(store, out_shape=jax.ShapeDtypeStruct(queries.shape, jnp.b...  1.35 us

profile of v3, /device:TPU:0, one launch (start us, length us, event | category | flops | bytes accessed | tf_op | source)
XLA Modules:
  0.0 44.0 jit_solution(4032648552615148398)
XLA Ops:
  0.7 42.0 %shard_map.91.held_ref = bf16[128,8192]{1,0:T(8,128)(2,1)S(1)} custom-call(bf16[128,8192]{1,0:T(8,128)(2,1)} %q_hbm.1, bf16[128,1024]{1,0:T(8,128)(2,1)} %nk_hbm.1, bf16[128,1024]{1,0:T(8,128)(2,1)} %nv_hbm.1, bf16[8,1024]{1,0:T(8,128)(2,1)} %pk_hbm.1, bf16[8,1024]{1,0:T(8,128)(2,1)} %pv_hbm.1, bf16[1,2,256,1024]{3,2,1,0:T(8,128)(2,1)} %poolk_hbm.1, ...), custom_call_target="tpu_custom_call" | custom-call | tf_op jit(solution)/shard_map/pallas_call | solution.py:516
  42.7 1.3 %shard_map.92 = bf16[128,8192]{1,0:T(8,128)(2,1)} custom-call(bf16[128,8192]{1,0:T(8,128)(2,1)S(1)} %shard_map.91.held_ref), custom_call_target="tpu_custom_call" | custom-call | tf_op jit(solution)/shard_map/pallas_call | solution.py:545

commit v4 on v3

--- a/solution.py
+++ b/solution.py
@@ -11,7 +11,9 @@
 CUTS = 1
 SIB = 1
 HOP = (3, 1)
-SUB = 4
+SUB = 2
+SCORE_SCALE = 1.4426950408889634 / HD**0.5
+DIMS = (((1,), (1,)), ((), ()))
 PRE_STEPS = (2, 5, 6)
 NEAR_STEP = 7
 STORES = 4
@@ -25,11 +27,46 @@
     return chips // short, short
 
 
+def cols(g):
+    return pl.ds(pl.multiple_of(g * HD, HD), HD)
+
+
+def with_ones(values):
+    return jnp.concatenate([values, jnp.ones_like(values)], axis=1)
+
+
+def query_rows(q_ref, head):
+    return jnp.concatenate([q_ref[:, cols(head + j)] for j in range(SUB)], axis=0)
+
+
+def attend(g, kv_heads, length, q_ref, kvf, near_sum, near_top, out_ref, first):
+    rows, group = q_ref.shape[0], q_ref.shape[1] // HD // kv_heads
+    pieces = kvf.shape[1] // kv_heads
+    all_rows = pieces * kvf.shape[2]
+    live = lax.broadcasted_iota(jnp.int32, (rows, HD), 0) < length
+    keys = kvf[0, pl.ds(g * pieces, pieces)].reshape(all_rows, HD)
+    values = with_ones(kvf[1, pl.ds(g * pieces, pieces)].reshape(all_rows, HD))
+    for sub in range(0, group, SUB):
+        scores = lax.dot_general(query_rows(q_ref, g * group + sub), keys, DIMS, preferred_element_type=jnp.float32)
+        part = pl.ds(sub * rows, SUB * rows)
+        before = near_top[g, part]
+        top = jnp.maximum(jnp.max(scores, axis=1, keepdims=True), before)
+        wide_top = jnp.concatenate([top] * (all_rows // HD), axis=1)
+        weights = jnp.exp2((scores - wide_top) * SCORE_SCALE).astype(jnp.bfloat16)
+        scale = jnp.exp2((before - top) * SCORE_SCALE)
+        summed = jnp.dot(weights, values, preferred_element_type=jnp.float32)
+        summed += jnp.concatenate([scale, scale], axis=1) * near_sum[g, part]
+        result = summed[:, :HD] / summed[:, HD:]
+        for j in range(SUB):
+            piece = jnp.where(live, result[j * rows : (j + 1) * rows], 0.0)
+            out_ref[:, cols(first + sub + j)] = piece.astype(out_ref.dtype)
+
+
 def kernel(
     ring, heads, kv_heads,
     q_hbm, nk_hbm, nv_hbm, pk_hbm, pv_hbm, poolk_hbm, poolv_hbm, owners_ref, lengths_ref,
-    out_ref,
-    page, pref, x, sib_s, sib_r, in_up, in_dn, up_s, up_r, dn_s, dn_r, kvf, bias, q_ref, nk_ref, nv_ref, near_sum, near_top,
+    out_ref, kvf, q_ref, near_sum, near_top,
+    page, pref, x, sib_s, sib_r, in_up, in_dn, up_s, up_r, dn_s, dn_r, bias, nk_ref, nv_ref,
     page_sems, load_sems, pre_send, pre_recv, send_sems, recv_sems,
 ):
     long, short = grid_of(ring)
@@ -165,9 +202,6 @@
             device_id={"ctx": target}, device_id_type=pl.DeviceIdType.MESH,
         )
 
-    def cols(g):
-        return pl.ds(pl.multiple_of(g * HD, HD), HD)
-
     def build(i):
         g, b = lax.div(i, pieces), lax.rem(i, pieces)
         page_of = lax.div(b, CUTS)
@@ -372,18 +406,6 @@
                 i = 2 * c + b
                 remote(5, b, i, kvf.at[core, i], kvf.at[1 - core, i], sibling).wait_recv()
 
-    live = lax.broadcasted_iota(jnp.int32, (rows, HD), 0) < length
-    score_scale = 1.4426950408889634 / HD**0.5
-    all_rows = pieces * blk
-
-    dims = (((1,), (1,)), ((), ()))
-
-    def with_ones(values):
-        return jnp.concatenate([values, jnp.ones_like(values)], axis=1)
-
-    def query_rows(head):
-        return jnp.concatenate([q_ref[:, cols(head + j)] for j in range(SUB)], axis=0)
-
     def near(g):
         keys = jnp.concatenate([pref[:, :, :, 0, :, cols(g)].reshape(pre, HD), nk_ref[:, cols(g)]], axis=0)
         values = jnp.concatenate([pref[:, :, :, 1, :, cols(g)].reshape(pre, HD), nv_ref[:, cols(g)]], axis=0)
@@ -391,30 +413,12 @@
         mask = jnp.concatenate([jnp.zeros((rows, pre), jnp.float32), bias[...]], axis=1)
         mask = jnp.concatenate([mask] * SUB, axis=0)
         for sub in range(0, group, SUB):
-            scores = lax.dot_general(query_rows(g * group + sub), keys, dims, preferred_element_type=jnp.float32) + mask
+            scores = lax.dot_general(query_rows(q_ref, g * group + sub), keys, DIMS, preferred_element_type=jnp.float32) + mask
             top = jnp.max(scores, axis=1, keepdims=True)
-            weights = jnp.exp2((scores - top) * score_scale).astype(jnp.bfloat16)
+            weights = jnp.exp2((scores - top) * SCORE_SCALE).astype(jnp.bfloat16)
             part = pl.ds(sub * rows, SUB * rows)
             near_sum[g, part] = jnp.dot(weights, values, preferred_element_type=jnp.float32)
             near_top[g, part] = jnp.broadcast_to(top, (SUB * rows, HD))
-
-    def attend(g):
-        keys = kvf[0, pl.ds(g * pieces, pieces)].reshape(all_rows, HD)
-        values = with_ones(kvf[1, pl.ds(g * pieces, pieces)].reshape(all_rows, HD))
-        for sub in range(0, group, SUB):
-            scores = lax.dot_general(query_rows(g * group + sub), keys, dims, preferred_element_type=jnp.float32)
-            part = pl.ds(sub * rows, SUB * rows)
-            before = near_top[g, part]
-            top = jnp.maximum(jnp.max(scores, axis=1, keepdims=True), before)
-            wide_top = jnp.concatenate([top] * (all_rows // HD), axis=1)
-            weights = jnp.exp2((scores - wide_top) * score_scale).astype(jnp.bfloat16)
-            scale = jnp.exp2((before - top) * score_scale)
-            summed = jnp.dot(weights, values, preferred_element_type=jnp.float32)
-            summed += jnp.concatenate([scale, scale], axis=1) * near_sum[g, part]
-            result = summed[:, :HD] / summed[:, HD:]
-            for j in range(SUB):
-                piece = jnp.where(live, result[j * rows : (j + 1) * rows], 0.0)
-                out_ref[:, cols(g * group + sub + j)] = piece.astype(out_ref.dtype)
 
     reach = max(root_hops(root) + max(root, short - 1 - root) for root in roots)
     done = SIB + after(reach + z_hops)
@@ -457,7 +461,10 @@
         @pl.when(at(u) & (lax.rem(u, per_head) == per_head - 1))
         def _():
             g = lax.div(u, per_head)
-            attend(g)
+
+            @pl.when(g < kv_heads - 1)
+            def _():
+                attend(g, kv_heads, length, q_ref, kvf, near_sum, near_top, out_ref, g * group)
 
         return carry
 
@@ -486,16 +493,25 @@
                 remote(kind, b, 0, x.at[half], sib_r.at[half], sibling).wait_send()
 
 
-def store(held_ref, out_hbm, sems):
-    rows = held_ref.shape[0] // STORES
-    copies = [
-        pltpu.make_async_copy(held_ref.at[pl.ds(n * rows, rows)], out_hbm.at[pl.ds(n * rows, rows)], sems.at[n])
+def finish(kv_heads, held_ref, kvf, q_ref, near_sum, near_top, lengths_ref, out_hbm, last_ref, sems):
+    rows, width = held_ref.shape
+    wide = width // kv_heads
+    ready = pl.ds(0, width - wide)
+    step = rows // STORES
+    stores = [
+        pltpu.make_async_copy(
+            held_ref.at[pl.ds(n * step, step), ready], out_hbm.at[pl.ds(n * step, step), ready], sems.at[n]
+        )
         for n in range(STORES)
     ]
-    for copy in copies:
-        copy.start()
-    for copy in copies:
-        copy.wait()
+    for store in stores:
+        store.start()
+    attend(kv_heads - 1, kv_heads, lengths_ref[0], q_ref, kvf, near_sum, near_top, last_ref, 0)
+    last = pltpu.make_async_copy(last_ref, out_hbm.at[:, pl.ds(width - wide, wide)], sems.at[STORES])
+    last.start()
+    for store in stores:
+        store.wait()
+    last.wait()
 
 
 def solution(mesh):
@@ -515,22 +531,24 @@
         vmem = pl.BlockSpec(memory_space=pltpu.VMEM)
         held = pl.pallas_call(
             functools.partial(kernel, ring, heads, kv_heads),
-            out_shape=pltpu.VMEM(queries.shape, jnp.bfloat16),
+            out_shape=(
+                pltpu.VMEM(queries.shape, jnp.bfloat16),
+                pltpu.VMEM((2, chunks, c_rows, HD), jnp.bfloat16),
+                pltpu.VMEM(queries.shape, jnp.bfloat16),
+                pltpu.VMEM((kv_heads, queries.shape[0] * heads // kv_heads, 2 * HD), jnp.float32),
+                pltpu.VMEM((kv_heads, queries.shape[0] * heads // kv_heads, HD), jnp.float32),
+            ),
             in_specs=[hbm] * 7 + [sm] * 2,
-            out_specs=vmem,
+            out_specs=(vmem,) * 5,
             scratch_shapes=[
                 pltpu.VMEM((2, pages, page_rows, kv_heads * HD), jnp.bfloat16),
                 pltpu.VMEM((2, long, short, 2) + prefix_keys.shape, jnp.bfloat16),
             ]
             + [chunk_buf] * 9
             + [
-                pltpu.VMEM((2, chunks, c_rows, HD), jnp.bfloat16),
                 pltpu.VMEM((queries.shape[0], queries.shape[0]), jnp.float32),
-                pltpu.VMEM(queries.shape, jnp.bfloat16),
                 pltpu.VMEM(new_keys.shape, jnp.bfloat16),
                 pltpu.VMEM(new_values.shape, jnp.bfloat16),
-                pltpu.VMEM((kv_heads, queries.shape[0] * heads // kv_heads, 2 * HD), jnp.float32),
-                pltpu.VMEM((kv_heads, queries.shape[0] * heads // kv_heads, HD), jnp.float32),
                 pltpu.SemaphoreType.DMA((2, 2)),
                 pltpu.SemaphoreType.DMA((5,)),
                 pltpu.SemaphoreType.DMA((short + long + 1,)),
@@ -539,17 +557,20 @@
                 pltpu.SemaphoreType.DMA((8, chunks)),
             ],
             compiler_params=pltpu.CompilerParams(
-                collective_id=0, has_side_effects=True, vmem_limit_bytes=56 * 2**20
+                collective_id=0, has_side_effects=True, vmem_limit_bytes=36 * 2**20
             ),
         )(queries, new_keys, new_values, prefix_keys, prefix_values, pool_keys, pool_values, owners, lengths)
         return pl.pallas_call(
-            store,
+            functools.partial(finish, kv_heads),
             out_shape=jax.ShapeDtypeStruct(queries.shape, jnp.bfloat16),
-            in_specs=[vmem],
+            in_specs=[vmem] * 5 + [sm],
             out_specs=hbm,
-            scratch_shapes=[pltpu.SemaphoreType.DMA((STORES,))],
-            compiler_params=pltpu.CompilerParams(vmem_limit_bytes=2**20),
-        )(held)
+            scratch_shapes=[
+                pltpu.VMEM((queries.shape[0], queries.shape[1] // kv_heads), jnp.bfloat16),
+                pltpu.SemaphoreType.DMA((STORES + 1,)),
+            ],
+            compiler_params=pltpu.CompilerParams(vmem_limit_bytes=16 * 2**20),
+        )(*held, lengths)
 
     two = P(("groups", "ctx"), None)
     four = P(("groups", "ctx"), None, None, None)

time: 44.2 us -> 43.3 us (0.980)
  Pallas kernels: 43.4 us -> 42.4 us
    pallas_call x1, Pallas kernels: 42 us -> 40.6 us  [body(): pl.pallas_call(functools.partial(kernel, ring, heads, kv_heads), out_shap...]
where the time goes in v4:
time: 43.3 us; the launch traced here: 43.1 us
  Pallas kernels  42.4 us (98%)
  between operations  0.66 us (2%)
    pallas_call x1, Pallas kernels, body(): pl.pallas_call(functools.partial(kernel, ring, heads, kv_heads), out_shap...  40.6 us
    pallas_call x1, Pallas kernels, body(): pl.pallas_call(functools.partial(finish, kv_heads), out_shape=jax.ShapeDt...  1.79 us

profile of v4, /device:TPU:0, one launch (start us, length us, event | category | flops | bytes accessed | tf_op | source)
XLA Modules:
  0.0 43.1 jit_solution(11309410530869420504)
XLA Ops:
  0.7 40.6 %shard_map.91 = (bf16[128,8192]{1,0:T(8,128)(2,1)S(1)}, bf16[2,16,256,128]{3,2,1,0:T(8,128)(2,1)S(1)}, bf16[128,8192]{1,0:T(8,128)(2,1)S(1)}, f32[8,1024,256]{2,1,0:T(8,128)S(1)}, f32[8,1024,128]{2,1,0:T(8,128)S(1)}) custom-call(bf16[128,8192]{1,0:T(8,128)(2,1)} %q_hbm.1, bf16[128,1024]{1,0:T(8,128)(2,1)} %nk_hbm.1, bf16[128,1024]{1,0:T(8,128)(2,1)} %nv_hbm.1, ...), custom_call_target="tpu_custom_call" | custom-call | tf_op jit(solution)/shard_map/pallas_call | solution.py:532
  41.3 1.8 %shard_map.92 = bf16[128,8192]{1,0:T(8,128)(2,1)} custom-call(bf16[128,8192]{1,0:T(8,128)(2,1)S(1)} %get-tuple-element.10.held_ref, bf16[2,16,256,128]{3,2,1,0:T(8,128)(2,1)S(1)} %get-tuple-element.11.kvf, bf16[128,8192]{1,0:T(8,128)(2,1)S(1)} %get-tuple-element.12.q_ref, f32[8,1024,256]{2,1,0:T(8,128)S(1)} %get-tuple-element.13.near_sum, ...), custom_call_target="tpu_custom_call" | custom-call | tf_op jit(solution)/shard_map/pallas_call | solution.py:563

commit v5 on v4

--- a/solution.py
+++ b/solution.py
@@ -151,50 +151,56 @@
         for slot in range(2):
             page_copy(poolk_hbm, slot, part).wait()
 
-    def pre_y(d, source):
+    def pre_copy(n, src, dst, target):
         return pltpu.make_async_remote_copy(
-            src_ref=mine, dst_ref=mine, send_sem=pre_send.at[source], recv_sem=pre_recv.at[source],
-            device_id={"ctx": y_peer(d)}, device_id_type=pl.DeviceIdType.MESH,
+            src_ref=src, dst_ref=dst, send_sem=pre_send.at[n], recv_sem=pre_recv.at[n],
+            device_id={"ctx": target}, device_id_type=pl.DeviceIdType.MESH,
         )
 
-    def pre_z(d, source):
-        row = pref.at[core, pz]
-        return pltpu.make_async_remote_copy(
-            src_ref=row, dst_ref=row, send_sem=pre_send.at[short + source], recv_sem=pre_recv.at[short + source],
-            device_id={"ctx": z_peer(d)}, device_id_type=pl.DeviceIdType.MESH,
-        )
+    def y_from(d):
+        return lax.rem(py + short - d, short)
+
+    def z_from(d):
+        return lax.rem(pz + long - d, long)
+
+    def pre_y(d):
+        return pre_copy(d, mine, mine, y_peer(d))
+
+    def pre_z(d):
+        return pre_copy(short + d, mine, mine, z_peer(d))
+
+    def pre_on(d, e):
+        block = pref.at[core, pz, y_from(e)]
+        return pre_copy(short + long + d * short + e, block, block, z_peer(d))
 
     def pre_sib(slot):
-        return pltpu.make_async_remote_copy(
-            src_ref=pref.at[slot], dst_ref=pref.at[slot], send_sem=pre_send.at[short + long], recv_sem=pre_recv.at[short + long],
-            device_id={"ctx": sibling}, device_id_type=pl.DeviceIdType.MESH,
-        )
+        return pre_copy(0, pref.at[slot], pref.at[slot], sibling)
 
     def pre_step(n):
         if n == 0:
-            for d in range(1, short):
-                pltpu.make_async_remote_copy(
-                    src_ref=mine, dst_ref=pref.at[core, pz, lax.rem(py + short - d, short)], send_sem=pre_send.at[d],
-                    recv_sem=pre_recv.at[d], device_id={"ctx": y_peer(d)}, device_id_type=pl.DeviceIdType.MESH,
-                ).wait_recv()
+            for e in range(1, short):
+                pre_copy(e, mine, pref.at[core, pz, y_from(e)], y_peer(e)).wait_recv()
             for d in range(1, long):
-                pre_z(d, d).start()
+                for e in range(1, short):
+                    pre_on(d, e).start()
         elif n == 1:
             for d in range(1, long):
-                pltpu.make_async_remote_copy(
-                    src_ref=pref.at[core, pz], dst_ref=pref.at[core, lax.rem(pz + long - d, long)], send_sem=pre_send.at[short + d],
-                    recv_sem=pre_recv.at[short + d], device_id={"ctx": z_peer(d)}, device_id_type=pl.DeviceIdType.MESH,
-                ).wait_recv()
+                pre_copy(short + d, mine, pref.at[core, z_from(d), py], z_peer(d)).wait_recv()
+                for e in range(1, short):
+                    n = short + long + d * short + e
+                    pre_copy(n, mine, pref.at[core, z_from(d), y_from(e)], z_peer(d)).wait_recv()
             pre_sib(core).start()
         else:
             pre_sib(1 - core).wait_recv()
 
     for load in own_pre:
         load.wait()
-    wait_pages(0)
     pl.semaphore_wait(barrier, peers)
     for d in range(1, short):
-        pre_y(d, d).start()
+        pre_y(d).start()
+    for d in range(1, long):
+        pre_z(d).start()
+    wait_pages(0)
 
     def remote(kind, b, i, src, dst, target):
         return pltpu.make_async_remote_copy(
@@ -471,9 +477,11 @@
     lax.fori_loop(0, steps, one_step, 0)
 
     for d in range(1, short):
-        pre_y(d, d).wait_send()
+        pre_y(d).wait_send()
     for d in range(1, long):
-        pre_z(d, d).wait_send()
+        pre_z(d).wait_send()
+        for e in range(1, short):
+            pre_on(d, e).wait_send()
     pre_sib(core).wait_send()
     half = pl.ds(0, pairs)
     every = pl.ds(0, chunks)
@@ -551,8 +559,8 @@
                 pltpu.VMEM(new_values.shape, jnp.bfloat16),
                 pltpu.SemaphoreType.DMA((2, 2)),
                 pltpu.SemaphoreType.DMA((5,)),
-                pltpu.SemaphoreType.DMA((short + long + 1,)),
-                pltpu.SemaphoreType.DMA((short + long + 1,)),
+                pltpu.SemaphoreType.DMA((short + long + long * short,)),
+                pltpu.SemaphoreType.DMA((short + long + long * short,)),
                 pltpu.SemaphoreType.DMA((8, 2)),
                 pltpu.SemaphoreType.DMA((8, chunks)),
             ],

time: 43.3 us -> 42 us (0.970)
  Pallas kernels: 42.4 us -> 41.1 us
    pallas_call x1, Pallas kernels: 40.6 us -> 39.3 us  [body(): pl.pallas_call(functools.partial(kernel, ring, heads, kv_heads), out_shap...]
where the time goes in v5:
time: 42 us; the launch traced here: 41.8 us
  Pallas kernels  41.1 us (98%)
  between operations  0.66 us (2%)
    pallas_call x1, Pallas kernels, body(): pl.pallas_call(functools.partial(kernel, ring, heads, kv_heads), out_shap...  39.3 us
    pallas_call x1, Pallas kernels, body(): pl.pallas_call(functools.partial(finish, kv_heads), out_shape=jax.ShapeDt...  1.79 us

profile of v5, /device:TPU:0, one launch (start us, length us, event | category | flops | bytes accessed | tf_op | source)
XLA Modules:
  0.0 41.8 jit_solution(13950014674740545717)
XLA Ops:
  0.7 39.3 %shard_map.91 = (bf16[128,8192]{1,0:T(8,128)(2,1)S(1)}, bf16[2,16,256,128]{3,2,1,0:T(8,128)(2,1)S(1)}, bf16[128,8192]{1,0:T(8,128)(2,1)S(1)}, f32[8,1024,256]{2,1,0:T(8,128)S(1)}, f32[8,1024,128]{2,1,0:T(8,128)S(1)}) custom-call(bf16[128,8192]{1,0:T(8,128)(2,1)} %q_hbm.1, bf16[128,1024]{1,0:T(8,128)(2,1)} %nk_hbm.1, bf16[128,1024]{1,0:T(8,128)(2,1)} %nv_hbm.1, ...), custom_call_target="tpu_custom_call" | custom-call | tf_op jit(solution)/shard_map/pallas_call | solution.py:540
  40.0 1.8 %shard_map.92 = bf16[128,8192]{1,0:T(8,128)(2,1)} custom-call(bf16[128,8192]{1,0:T(8,128)(2,1)S(1)} %get-tuple-element.10.held_ref, bf16[2,16,256,128]{3,2,1,0:T(8,128)(2,1)S(1)} %get-tuple-element.11.kvf, bf16[128,8192]{1,0:T(8,128)(2,1)S(1)} %get-tuple-element.12.q_ref, f32[8,1024,256]{2,1,0:T(8,128)S(1)} %get-tuple-element.13.near_sum, ...), custom_call_target="tpu_custom_call" | custom-call | tf_op jit(solution)/shard_map/pallas_call | solution.py:571
